TPU v7x, 32 devices: a whole 2x2x4 slice. The times are simulated.
32 devices in a mesh: row: 8 (over y, x, core), col: 4 (over z).
Axes of the slice: x: 2, y: 2, z: 4, core: 2. Of those that a mesh axis runs over, the one named last changes fastest.
Arguments:
- vector_panel: bfloat16 [8192, 256], P(('row', 'col')), may hold values from -6 to 6
- block_tiles: bfloat16 [3072, 128, 128], P(('row', 'col')), may hold values from -0.0625 to 0.0625
- tile_rows: int32 [3072], P(('row', 'col')), may hold values from 0 to 63, as said below
- tile_cols: int32 [3072], P(('row', 'col')), may hold values from 0 to 63, as said below
- owner_counts: int32 [32], P(('row', 'col')), may hold values from 1 to 96, as said below
Outputs:
- filtered: bfloat16 [8192, 256], P(('row', 'col'))
Inputs may be any that keep to these rules, and one draw needn't show every extreme that they name: The live slots of owner (row index p, col index q) hold distinct pairs (tile_rows, tile_cols) with tile_rows <= tile_cols, tile_rows in p * 2 * 4 to (p + 1) * 2 * 4 - 1 and tile_cols // 2 % 4 = q; slots past the owner's count repeat its first pair and are ignored. `tile_cols`: see tile_rows. `owner_counts`: some owner fills all 96 slots.
All inputs are finite; a program needn't handle non-finite values.
Results may differ from a plain program's by a relative error of at most 0.022.
Values may be sent and summed in bfloat16 or wider, within the bound.
No kernel may reach another device: no remote copies, remote signals or barrier semaphores. Data moves between devices by JAX's collectives and lax.ppermute only.
A program may use at most 128 MiB of HBM per device.

v0:
```python
import jax
import jax.numpy as jnp
from jax import lax
from jax.sharding import PartitionSpec as P

BS = 128
center_shift = 0.25
half_width = 1.25


def apply_blocks(
    panel, block_tiles, row_slot, set_slot, row_select, set_select, range_blocks, set_blocks
):
    width = panel.shape[1]
    gathered_set = lax.all_gather(panel, "row", axis=0, tiled=True).reshape(set_blocks, BS, width)
    picked_set = jnp.take(gathered_set, set_slot, axis=0)
    upper = jnp.einsum("sij,sjw->siw", block_tiles, picked_set, preferred_element_type=jnp.float32)
    upper_sum = jnp.einsum(
        "as,siw->aiw", row_select, upper, precision=lax.Precision.HIGHEST
    ).astype(jnp.bfloat16)
    own_upper = lax.psum_scatter(
        upper_sum.reshape(range_blocks * BS, width), "col", scatter_dimension=0, tiled=True
    ).astype(jnp.float32)
    gathered_range = lax.all_gather(panel, "col", axis=0, tiled=True).reshape(
        range_blocks, BS, width
    )
    picked_range = jnp.take(gathered_range, row_slot, axis=0)
    lower = jnp.einsum(
        "sji,sjw->siw", block_tiles, picked_range, preferred_element_type=jnp.float32
    )
    lower_sum = jnp.einsum(
        "bs,siw->biw", set_select, lower, precision=lax.Precision.HIGHEST
    ).astype(jnp.bfloat16)
    own_lower = lax.psum_scatter(
        lower_sum.reshape(set_blocks * BS, width), "row", scatter_dimension=0, tiled=True
    ).astype(jnp.float32)
    return own_upper + own_lower


def per_device(vector_panel, block_tiles, tile_rows, tile_cols, owner_counts):
    n_rows = lax.axis_size("row")
    n_cols = lax.axis_size("col")
    row_index = lax.axis_index("row")
    panel_blocks = vector_panel.shape[0] // BS
    slots = block_tiles.shape[0]
    range_blocks = panel_blocks * n_cols
    set_blocks = panel_blocks * n_rows
    row_slot = tile_rows - row_index * range_blocks
    shard_of = tile_cols // panel_blocks
    set_slot = shard_of // n_cols * panel_blocks + tile_cols % panel_blocks
    live_slots = jnp.arange(slots, dtype=jnp.int32) < owner_counts[0]
    row_select = (
        (row_slot[None, :] == jnp.arange(range_blocks, dtype=jnp.int32)[:, None])
        & live_slots[None, :]
    ).astype(jnp.float32)
    set_select = (
        (set_slot[None, :] == jnp.arange(set_blocks, dtype=jnp.int32)[:, None])
        & live_slots[None, :]
    ).astype(jnp.float32)

    def operate(panel):
        return apply_blocks(
            panel, block_tiles, row_slot, set_slot, row_select, set_select, range_blocks, set_blocks
        )

    start_f = vector_panel.astype(jnp.float32)
    hx = operate(vector_panel)
    first_step = ((hx - center_shift * start_f) / half_width).astype(jnp.bfloat16)
    first_f = first_step.astype(jnp.float32)
    hfirst = operate(first_step)
    filtered = 2.0 * (hfirst - center_shift * first_f) / half_width - start_f
    return filtered.astype(jnp.bfloat16)


def solution(mesh):
    in_specs = (
        P(("row", "col"), None),
        P(("row", "col"), None, None),
        P(("row", "col")),
        P(("row", "col")),
        P(("row", "col")),
    )
    out_specs = P(("row", "col"), None)
    return jax.shard_map(
        per_device, mesh=mesh, in_specs=in_specs, out_specs=out_specs, check_vma=False
    )
```

profile of v0, /device:TPU:0, one launch (start us, length us, event | category | flops | bytes accessed | tf_op | source)
XLA Modules:
  0.0 249.5 jit_solution(10400839575763858375)
XLA Ops:
  6.5 0.7 all-gather.3.cloned.1.call-update
  7.3 0.8 compare_and_fusion.1
  8.1 19.4 %all_gather.13 = bf16[1024,256]{1,0:T(8,128)(2,1)} all-gather(bf16[256,256]{1,0:T(8,128)(2,1)} %param.9), channel_id=1, replica_groups=mesh['row'=8,'col'=4] {'col'}, dimensions={0}, use_global_device_ids=true | all-gather | bytes 655360 | tf_op jit(solution)/shard_map/all_gather | solution.py:24
  27.5 7.0 %gather_fusion.1 = bf16[96,128,256]{2,1,0:T(8,128)(2,1)} fusion(bf16[8,128,256]{2,1,0:T(8,128)(2,1)} %bitcast.42, s32[1024]{0:T(1024)S(1)} %pad_clamp_fusion), kind=kCustom, calls=%fused_computation.1.clone | custom fusion | bytes 12583296 | tf_op jit(solution)/shard_map/jit(_take)/gather | solution.py:27
  34.5 9.3 %fusion.12 = f32[96,256,128]{2,1,0:T(8,128)} fusion(bf16[96,128,128]{2,1,0:T(8,128)(2,1)S(1)} %copy-done, bf16[96,128,256]{2,1,0:T(8,128)(2,1)} %gather_fusion.1, pred[96]{0:T(512)(128)(4,1)S(1)} %get-tuple-element.9), kind=kOutput, calls=%fused_computation.16 | convolution fusion | flops 808452096 | bytes 22020192 | tf_op jit(solution)/shard_map/sji,sjw->siw/dot_general | solution.py:28
  43.8 12.7 %copy.11 = f32[96,256,128]{1,0,2:T(8,128)} copy(f32[96,256,128]{2,1,0:T(8,128)} %fusion.12) | data formatting | bytes 25165824 | tf_op jit(solution)/shard_map/sji,sjw->siw/dot_general | solution.py:28
  57.2 7.1 %fusion.24 = bf16[16,128,256]{2,0,1:T(8,128)(2,1)S(1)} fusion(f32[96,256,128]{1,0,2:T(8,128)} %copy.11, s32[96]{0:T(128)S(1)} %get-tuple-element.8, pred[96]{0:T(512)(128)(4,1)S(1)} %iota_compare_fusion.2), kind=kOutput, calls=%fused_computation.28 | convolution fusion | flops 604507136 | bytes 13631968 | tf_op jit(solution)/shard_map/bs,siw->biw/dot_general | solution.py:31
  64.3 1.3 copy.7
  65.7 0.2 reduce-scatter.5.cloned.1.call-start
  65.9 7.3 %gather_fusion = bf16[96,128,256]{2,1,0:T(8,128)(2,1)} fusion(bf16[16,128,256]{2,1,0:T(8,128)(2,1)} %bitcast.44, s32[1024]{0:T(1024)S(1)} %pad_clamp_fusion.1), kind=kCustom, calls=%fused_computation.clone | custom fusion | bytes 12583296 | tf_op jit(solution)/shard_map/jit(_take)/gather | solution.py:16
  73.2 9.5 %fusion.14 = f32[96,256,128]{2,1,0:T(8,128)} fusion(bf16[96,128,128]{2,1,0:T(8,128)(2,1)S(1)} %copy-done, bf16[96,128,256]{2,1,0:T(8,128)(2,1)} %gather_fusion, pred[96]{0:T(512)(128)(4,1)S(1)} %get-tuple-element.6), kind=kOutput, calls=%fused_computation.18 | convolution fusion | flops 808452096 | bytes 22020192 | tf_op jit(solution)/shard_map/sij,sjw->siw/dot_general | solution.py:17
  82.7 12.7 %copy.10 = f32[96,256,128]{1,0,2:T(8,128)} copy(f32[96,256,128]{2,1,0:T(8,128)} %fusion.14) | data formatting | bytes 25165824 | tf_op jit(solution)/shard_map/sij,sjw->siw/dot_general | solution.py:17
  95.4 7.1 %fusion.30 = bf16[8,128,256]{2,0,1:T(8,128)(2,1)S(1)} fusion(f32[96,256,128]{1,0,2:T(8,128)} %copy.10, s32[96]{0:T(128)S(1)} %get-tuple-element.10, pred[96]{0:T(512)(128)(4,1)S(1)} %iota_compare_fusion.2), kind=kOutput, calls=%fused_computation.30 | convolution fusion | flops 302253568 | bytes 13107680 | tf_op jit(solution)/shard_map/as,siw->aiw/dot_general | solution.py:18
  102.6 0.9 copy.6
  103.5 0.0 all-gather.5.cloned.1.call-start
  103.6 22.1 %reduce-scatter.5.cloned.1.call-done = bf16[256,256]{1,0:T(8,128)(2,1)} async-done(((bf16[1024,256]{1,0:T(8,128)(2,1)}), bf16[256,256]{1,0:T(8,128)(2,1)}) %reduce-scatter.5.cloned.1.call-update) | async-done | bytes 131088 | tf_op jit(solution)/shard_map/reduce_scatter | solution.py:21
  125.6 1.7 fusion.38
  127.4 0.0 reduce-scatter.11.cloned.1.call-start
  127.4 17.2 %all_gather.15 = bf16[1024,256]{1,0:T(8,128)(2,1)} all-gather(bf16[256,256]{1,0:T(8,128)(2,1)} %fusion.38), channel_id=1, replica_groups=mesh['row'=8,'col'=4] {'col'}, dimensions={0}, use_global_device_ids=true | all-gather | bytes 655360 | tf_op jit(solution)/shard_map/all_gather | solution.py:24
  144.6 7.0 %gather_fusion.3 = bf16[96,128,256]{2,1,0:T(8,128)(2,1)} fusion(bf16[8,128,256]{2,1,0:T(8,128)(2,1)} %bitcast.43, s32[1024]{0:T(1024)S(1)} %pad_clamp_fusion), kind=kCustom, calls=%fused_computation.3.clone | custom fusion | bytes 12583296 | tf_op jit(solution)/shard_map/jit(_take)/gather | solution.py:27
  151.5 9.3 %fusion.8 = f32[96,256,128]{2,1,0:T(8,128)} fusion(bf16[96,128,128]{2,1,0:T(8,128)(2,1)S(1)} %copy-done, bf16[96,128,256]{2,1,0:T(8,128)(2,1)} %gather_fusion.3, pred[96]{0:T(512)(128)(4,1)S(1)} %get-tuple-element.9), kind=kOutput, calls=%fused_computation.12 | convolution fusion | flops 808452096 | bytes 22020192 | tf_op jit(solution)/shard_map/sji,sjw->siw/dot_general | solution.py:28
  160.8 12.7 %copy.13 = f32[96,256,128]{1,0,2:T(8,128)} copy(f32[96,256,128]{2,1,0:T(8,128)} %fusion.8) | data formatting | bytes 25165824 | tf_op jit(solution)/shard_map/sji,sjw->siw/dot_general | solution.py:28
  173.5 7.1 %fusion.27 = bf16[16,128,256]{2,0,1:T(8,128)(2,1)S(1)} fusion(f32[96,256,128]{1,0,2:T(8,128)} %copy.13, s32[96]{0:T(128)S(1)} %get-tuple-element.8, pred[96]{0:T(512)(128)(4,1)S(1)} %iota_compare_fusion.2), kind=kOutput, calls=%fused_computation.29 | convolution fusion | flops 604507136 | bytes 13631968 | tf_op jit(solution)/shard_map/bs,siw->biw/dot_general | solution.py:31
  180.6 1.3 copy.9
  182.0 0.3 reduce-scatter.9.cloned.1.call-start
  182.3 7.3 %gather_fusion.2 = bf16[96,128,256]{2,1,0:T(8,128)(2,1)} fusion(bf16[16,128,256]{2,1,0:T(8,128)(2,1)} %bitcast.45, s32[1024]{0:T(1024)S(1)} %pad_clamp_fusion.1), kind=kCustom, calls=%fused_computation.2.clone | custom fusion | bytes 12583296 | tf_op jit(solution)/shard_map/jit(_take)/gather | solution.py:16
  189.6 9.5 %fusion.10 = f32[96,256,128]{2,1,0:T(8,128)} fusion(bf16[96,128,128]{2,1,0:T(8,128)(2,1)S(1)} %copy-done, bf16[96,128,256]{2,1,0:T(8,128)(2,1)} %gather_fusion.2, pred[96]{0:T(512)(128)(4,1)S(1)} %get-tuple-element.6), kind=kOutput, calls=%fused_computation.14 | convolution fusion | flops 808452096 | bytes 22020192 | tf_op jit(solution)/shard_map/sij,sjw->siw/dot_general | solution.py:17
  199.0 12.7 %copy.12 = f32[96,256,128]{1,0,2:T(8,128)} copy(f32[96,256,128]{2,1,0:T(8,128)} %fusion.10) | data formatting | bytes 25165824 | tf_op jit(solution)/shard_map/sij,sjw->siw/dot_general | solution.py:17
  211.7 7.1 %fusion.33 = bf16[8,128,256]{2,0,1:T(8,128)(2,1)S(1)} fusion(f32[96,256,128]{1,0,2:T(8,128)} %copy.12, s32[96]{0:T(128)S(1)} %get-tuple-element.10, pred[96]{0:T(512)(128)(4,1)S(1)} %iota_compare_fusion.2), kind=kOutput, calls=%fused_computation.31 | convolution fusion | flops 302253568 | bytes 13107680 | tf_op jit(solution)/shard_map/as,siw->aiw/dot_general | solution.py:18
  218.8 0.9 copy.8
  219.8 21.2 %reduce-scatter.9.cloned.1.call-done = bf16[256,256]{1,0:T(8,128)(2,1)} async-done(((bf16[1024,256]{1,0:T(8,128)(2,1)}), bf16[256,256]{1,0:T(8,128)(2,1)}) %reduce-scatter.9.cloned.1.call-update) | async-done | bytes 131088 | tf_op jit(solution)/shard_map/reduce_scatter | solution.py:21
  241.0 1.7 fusion.39
  (25 shorter events, 0.3 us)
Async XLA Ops:
  6.5 28.0 %copy-start = (bf16[96,128,128]{2,1,0:T(8,128)(2,1)S(1)}, bf16[96,128,128]{2,1,0:T(8,128)(2,1)}, u32[]{:S(2)}) copy-start(bf16[96,128,128]{2,1,0:T(8,128)(2,1)} %param.10) | copy-start | bytes 9437188
  6.5 59.4 %all-gather.3.cloned.1.call-start = ((), (), s32[]{:S(2)}) async-start(), calls=%async_computation.4 | async-start | bytes 1179648 | tf_op jit(solution)/shard_map/all_gather | solution.py:15
  7.3 96.3 %reduce-scatter.7.cloned.1.call-start = ((), (), s32[]{:S(2)}) async-start(), calls=%async_computation.6 | async-start | bytes 1179648 | tf_op jit(solution)/shard_map/reduce_scatter | solution.py:34
  43.8 13.4 %copy-start.3 = (s32[96]{0:T(128)S(1)}, s32[96]{0:T(128)}, u32[]{:S(2)}) copy-start(s32[96]{0:T(128)} %param.12) | copy-start | bytes 1156
  65.7 60.0 %reduce-scatter.5.cloned.1.call-start = ((), (), s32[]{:S(2)}) async-start(), calls=%async_computation.5 | async-start | bytes 655360 | tf_op jit(solution)/shard_map/reduce_scatter | solution.py:21
  95.4 30.2 %copy-start.1 = (bf16[256,256]{1,0:T(8,128)(2,1)S(1)}, bf16[256,256]{1,0:T(8,128)(2,1)}, u32[]{:S(2)}) copy-start(bf16[256,256]{1,0:T(8,128)(2,1)} %param.9) | copy-start | bytes 393220
  103.5 78.8 %all-gather.5.cloned.1.call-start = ((), (), s32[]{:S(2)}) async-start(), calls=%async_computation.7 | async-start | bytes 1179648 | tf_op jit(solution)/shard_map/all_gather | solution.py:15
  127.4 92.4 %reduce-scatter.11.cloned.1.call-start = ((), (), s32[]{:S(2)}) async-start(), calls=%async_computation.9 | async-start | bytes 1179648 | tf_op jit(solution)/shard_map/reduce_scatter | solution.py:34
  182.0 59.0 %reduce-scatter.9.cloned.1.call-start = ((), (), s32[]{:S(2)}) async-start(), calls=%async_computation.8 | async-start | bytes 655360 | tf_op jit(solution)/shard_map/reduce_scatter | solution.py:21
  211.7 29.2 %copy-start.2 = (bf16[256,256]{1,0:T(8,128)(2,1)S(1)}, bf16[256,256]{1,0:T(8,128)(2,1)}, u32[]{:S(2)}) copy-start(bf16[256,256]{1,0:T(8,128)(2,1)} %fusion.38) | copy-start | bytes 393220
Sparse Core Ops, SparseCore 0:
  9.2 26.0 all-gather.2
  65.8 35.6 reduce-scatter.6
  103.8 21.8 reduce-scatter.4
  127.5 21.6 all-gather.4
  182.1 34.8 reduce-scatter.10
  219.9 21.0 reduce-scatter.8
where the time goes:
time: 251 us; the launch traced here: 250 us
  local copies, waits for them, and re-layouts  83.9 us (33%)
  matrix products  65.8 us (26%)
  waiting for transfers between devices  44.1 us (18%)
  blocking collectives  36.5 us (15%)
  between operations  14.2 us (6%)
  other arithmetic  4.28 us (2%)
    reduce_scatter x2, waiting for transfers between devices, apply_blocks(): lax.psum_scatter(upper_sum.reshape(range_blocks * BS, width), 'col', scat...  43.3 us
    all_gather x2, blocking collectives, apply_blocks(): lax.all_gather(panel, 'col', axis=0, tiled=True)  36.5 us
    dot_general x2, local copies, waits for them, and re-layouts, apply_blocks(): jnp.einsum('sij,sjw->siw', block_tiles, picked_set, preferred_element_typ...  25.5 us
    dot_general x2, local copies, waits for them, and re-layouts, apply_blocks(): jnp.einsum('sji,sjw->siw', block_tiles, picked_range, preferred_element_t...  25.4 us
    dot_general x2, matrix products, apply_blocks(): jnp.einsum('sij,sjw->siw', block_tiles, picked_set, preferred_element_typ...  18.9 us
    dot_general x2, matrix products, apply_blocks(): jnp.einsum('sji,sjw->siw', block_tiles, picked_range, preferred_element_t...  18.5 us
    gather x2, local copies, waits for them, and re-layouts, apply_blocks(): picked_set = jnp.take(gathered_set, set_slot, axis=0)  14.5 us
    dot_general x2, matrix products, apply_blocks(): jnp.einsum('as,siw->aiw', row_select, upper, precision=lax.Precision.HIGH...  14.2 us
  transfers between devices with their start and end apart: 6, of which 2 were waited for; matrix products, arithmetic and copies ran while one was open for 60% of the time, Pallas kernels for 0%

commit v1 on v0

--- a/solution.py
+++ b/solution.py
@@ -6,6 +6,27 @@
 BS = 128
 center_shift = 0.25
 half_width = 1.25
+
+
+def gather_around(x, axis, dim):
+    size, place, rows = (lax.axis_size(axis), lax.axis_index(axis), x.shape[dim])
+    ahead = [(i, (i + 1) % size) for i in range(size)]
+    left = [(i, (i - 1) % size) for i in range(size)]
+    result = jnp.zeros((*x.shape[:dim], size * rows, *x.shape[dim + 1 :]), x.dtype)
+    result = lax.dynamic_update_slice_in_dim(result, x, place * rows, axis=dim)
+    from_left = from_right = x
+    half = size // 2
+    for step in range(1, half + 1):
+        from_left = lax.ppermute(from_left, axis, ahead)
+        result = lax.dynamic_update_slice_in_dim(
+            result, from_left, (place - step) % size * rows, axis=dim
+        )
+        if step < size - half:
+            from_right = lax.ppermute(from_right, axis, left)
+            result = lax.dynamic_update_slice_in_dim(
+                result, from_right, (place + step) % size * rows, axis=dim
+            )
+    return result
 
 
 def apply_blocks(
@@ -21,9 +42,7 @@
     own_upper = lax.psum_scatter(
         upper_sum.reshape(range_blocks * BS, width), "col", scatter_dimension=0, tiled=True
     ).astype(jnp.float32)
-    gathered_range = lax.all_gather(panel, "col", axis=0, tiled=True).reshape(
-        range_blocks, BS, width
-    )
+    gathered_range = gather_around(panel, "col", 0).reshape(range_blocks, BS, width)
     picked_range = jnp.take(gathered_range, row_slot, axis=0)
     lower = jnp.einsum(
         "sji,sjw->siw", block_tiles, picked_range, preferred_element_type=jnp.float32

time: 251 us -> 243 us (0.968)
  blocking collectives: 36.5 us -> 0 us
  waiting for transfers between devices: 44.1 us -> 56.1 us
  starting transfers between devices: 0.65 us -> 9.02 us
  local copies, waits for them, and re-layouts: 83.9 us -> 91.9 us
    all_gather x2 -> x0, blocking collectives: 36.5 us -> none  [apply_blocks(): lax.all_gather(panel, 'col', axis=0, tiled=True)]
    ppermute x0 -> x6, waiting for transfers between devices: none -> 13.9 us  [the longest x4 13.3 us: gather_around(): from_left = lax.ppermute(from_left, axis, ahead)]
    ppermute x0 -> x6, starting transfers between devices: none -> 8.37 us  [the longest x2 5.25 us: gather_around(): from_right = lax.ppermute(from_right, axis, left)]
    dynamic_update_slice x0 -> x7, local copies, waits for them, and re-layouts: none -> 5.56 us  [the longest x4 2.67 us: gather_around(): lax.dynamic_update_slice_in_dim(result, from_left, (place - step) % size...]
  transfers between devices with their start and end apart: 6 -> 12, of which waited for: 2 -> 6; matrix products, arithmetic and copies ran while one was open for 60% -> 65% of each run, Pallas kernels for 0% -> 0%
where the time goes in v1:
time: 243 us; the launch traced here: 242 us
  local copies, waits for them, and re-layouts  91.9 us (38%)
  matrix products  65.8 us (27%)
  waiting for transfers between devices  56.1 us (23%)
  between operations  14.3 us (6%)
  starting transfers between devices  9.02 us (4%)
  other arithmetic  4.77 us (2%)
    reduce_scatter x2, waiting for transfers between devices, apply_blocks(): lax.psum_scatter(upper_sum.reshape(range_blocks * BS, width), 'col', scat...  42.1 us
    dot_general x2, local copies, waits for them, and re-layouts, apply_blocks(): jnp.einsum('sij,sjw->siw', block_tiles, picked_set, preferred_element_typ...  25.6 us
    dot_general x2, local copies, waits for them, and re-layouts, apply_blocks(): jnp.einsum('sji,sjw->siw', block_tiles, picked_range, preferred_element_t...  25.5 us
    dot_general x2, matrix products, apply_blocks(): jnp.einsum('sij,sjw->siw', block_tiles, picked_set, preferred_element_typ...  18.9 us
    dot_general x2, matrix products, apply_blocks(): jnp.einsum('sji,sjw->siw', block_tiles, picked_range, preferred_element_t...  18.6 us
    gather x2, local copies, waits for them, and re-layouts, apply_blocks(): picked_set = jnp.take(gathered_set, set_slot, axis=0)  14.5 us
    dot_general x2, matrix products, apply_blocks(): jnp.einsum('as,siw->aiw', row_select, upper, precision=lax.Precision.HIGH...  14.2 us
    dot_general x2, matrix products, apply_blocks(): jnp.einsum('bs,siw->biw', set_select, lower, precision=lax.Precision.HIGH...  14.2 us
  transfers between devices with their start and end apart: 12, of which 6 were waited for; matrix products, arithmetic and copies ran while one was open for 65% of the time, Pallas kernels for 0%

profile of v1, /device:TPU:0, one launch (start us, length us, event | category | flops | bytes accessed | tf_op | source)
XLA Modules:
  0.0 241.9 jit_solution(5096583621111312540)
XLA Ops:
  6.5 3.1 %collective-permute-start = (bf16[256,256]{1,0:T(8,128)(2,1)}, bf16[256,256]{1,0:T(8,128)(2,1)S(1)}, u32[]{:S(2)}, u32[]{:S(2)}) collective-permute-start(bf16[256,256]{1,0:T(8,128)(2,1)} %param.9), channel_id=1, source_target_pairs={{0,1},{1,2},{2,3},{3,0},{4,5},{5,6},{6,7},{7,4},{8,9},{9,10},{10,1... | collective-permute-start | bytes 393224 | tf_op jit(solution)/shard_map/ppermute | solution.py:20
  9.6 2.0 collective-permute-start.1
  13.1 0.8 broadcast.47.clone
  13.9 1.6 constant_dynamic-update-slice_fusion.7
  18.2 4.8 %collective-permute-done.2 = bf16[256,256]{1,0:T(8,128)(2,1)S(1)} collective-permute-done((bf16[256,256]{1,0:T(8,128)(2,1)S(1)}, bf16[256,256]{1,0:T(8,128)(2,1)S(1)}, u32[]{:S(2)}, u32[]{:S(2)}) %collective-permute-start.2) | collective-permute-done | bytes 131104 | tf_op jit(solution)/shard_map/ppermute | solution.py:20
  23.7 7.0 %gather_fusion.1 = bf16[96,128,256]{2,1,0:T(8,128)(2,1)} fusion(bf16[8,128,256]{2,1,0:T(8,128)(2,1)} %bitcast.6, s32[1024]{0:T(1024)S(1)} %pad_clamp_fusion), kind=kCustom, calls=%fused_computation.1.clone | custom fusion | bytes 12583296 | tf_op jit(solution)/shard_map/jit(_take)/gather | solution.py:46
  30.7 9.3 %fusion.12 = f32[96,256,128]{2,1,0:T(8,128)} fusion(bf16[96,128,128]{2,1,0:T(8,128)(2,1)S(1)} %copy-done, bf16[96,128,256]{2,1,0:T(8,128)(2,1)} %gather_fusion.1, pred[96]{0:T(512)(128)(4,1)S(1)} %get-tuple-element.11), kind=kOutput, calls=%fused_computation.16 | convolution fusion | flops 808452096 | bytes 22020192 | tf_op jit(solution)/shard_map/sji,sjw->siw/dot_general | solution.py:47
  40.0 12.7 %copy.11 = f32[96,256,128]{1,0,2:T(8,128)} copy(f32[96,256,128]{2,1,0:T(8,128)} %fusion.12) | data formatting | bytes 25165824 | tf_op jit(solution)/shard_map/sji,sjw->siw/dot_general | solution.py:47
  52.7 7.1 %fusion.24 = bf16[16,128,256]{2,0,1:T(8,128)(2,1)S(1)} fusion(f32[96,256,128]{1,0,2:T(8,128)} %copy.11, s32[96]{0:T(128)S(1)} %get-tuple-element.10, pred[96]{0:T(512)(128)(4,1)S(1)} %iota_compare_fusion.2), kind=kOutput, calls=%fused_computation.28 | convolution fusion | flops 604507136 | bytes 13631968 | tf_op jit(solution)/shard_map/bs,siw->biw/dot_general | solution.py:50
  59.8 1.4 copy.7
  61.4 7.3 %gather_fusion = bf16[96,128,256]{2,1,0:T(8,128)(2,1)} fusion(bf16[16,128,256]{2,1,0:T(8,128)(2,1)} %bitcast.42, s32[1024]{0:T(1024)S(1)} %pad_clamp_fusion.1), kind=kCustom, calls=%fused_computation.clone | custom fusion | bytes 12583296 | tf_op jit(solution)/shard_map/jit(_take)/gather | solution.py:37
  68.7 9.4 %fusion.14 = f32[96,256,128]{2,1,0:T(8,128)} fusion(bf16[96,128,128]{2,1,0:T(8,128)(2,1)S(1)} %copy-done, bf16[96,128,256]{2,1,0:T(8,128)(2,1)} %gather_fusion, pred[96]{0:T(512)(128)(4,1)S(1)} %get-tuple-element.9), kind=kOutput, calls=%fused_computation.18 | convolution fusion | flops 808452096 | bytes 22020192 | tf_op jit(solution)/shard_map/sij,sjw->siw/dot_general | solution.py:38
  78.2 12.8 %copy.10 = f32[96,256,128]{1,0,2:T(8,128)} copy(f32[96,256,128]{2,1,0:T(8,128)} %fusion.14) | data formatting | bytes 25165824 | tf_op jit(solution)/shard_map/sij,sjw->siw/dot_general | solution.py:38
  90.9 7.1 %fusion.30 = bf16[8,128,256]{2,0,1:T(8,128)(2,1)S(1)} fusion(f32[96,256,128]{1,0,2:T(8,128)} %copy.10, s32[96]{0:T(128)S(1)} %get-tuple-element.12, pred[96]{0:T(512)(128)(4,1)S(1)} %iota_compare_fusion.2), kind=kOutput, calls=%fused_computation.30 | convolution fusion | flops 302253568 | bytes 13107680 | tf_op jit(solution)/shard_map/as,siw->aiw/dot_general | solution.py:39
  98.1 0.9 copy.6
  99.1 21.7 %reduce-scatter.5.cloned.1.call-done = bf16[256,256]{1,0:T(8,128)(2,1)} async-done(((bf16[1024,256]{1,0:T(8,128)(2,1)}), bf16[256,256]{1,0:T(8,128)(2,1)}) %reduce-scatter.5.cloned.1.call-update) | async-done | bytes 131088 | tf_op jit(solution)/shard_map/reduce_scatter | solution.py:42
  121.6 1.7 constant_dynamic-update-slice_fusion.3
  124.1 3.2 %collective-permute-start.4 = (bf16[256,256]{1,0:T(8,128)(2,1)}, bf16[256,256]{1,0:T(8,128)(2,1)S(1)}, u32[]{:S(2)}, u32[]{:S(2)}) collective-permute-start(bf16[256,256]{1,0:T(8,128)(2,1)} %copy-done.2), channel_id=1, source_target_pairs={{0,3},{1,0},{2,1},{3,2},{4,7},{5,4},{6,5},{7,6},{8,11},{9,8},{10,9... | collective-permute-start | bytes 393224 | tf_op jit(solution)/shard_map/ppermute | solution.py:25
  127.3 3.0 %collective-permute-done.3 = bf16[256,256]{1,0:T(8,128)(2,1)S(1)} collective-permute-done((bf16[256,256]{1,0:T(8,128)(2,1)S(1)}, bf16[256,256]{1,0:T(8,128)(2,1)S(1)}, u32[]{:S(2)}, u32[]{:S(2)}) %collective-permute-start.3) | collective-permute-done | bytes 131104 | tf_op jit(solution)/shard_map/ppermute | solution.py:20
  131.6 5.4 %collective-permute-done.5 = bf16[256,256]{1,0:T(8,128)(2,1)S(1)} collective-permute-done((bf16[256,256]{1,0:T(8,128)(2,1)S(1)}, bf16[256,256]{1,0:T(8,128)(2,1)S(1)}, u32[]{:S(2)}, u32[]{:S(2)}) %collective-permute-start.5) | collective-permute-done | bytes 131104 | tf_op jit(solution)/shard_map/ppermute | solution.py:20
  137.7 7.0 %gather_fusion.3 = bf16[96,128,256]{2,1,0:T(8,128)(2,1)} fusion(bf16[8,128,256]{2,1,0:T(8,128)(2,1)} %bitcast.12, s32[1024]{0:T(1024)S(1)} %pad_clamp_fusion), kind=kCustom, calls=%fused_computation.3.clone | custom fusion | bytes 12583296 | tf_op jit(solution)/shard_map/jit(_take)/gather | solution.py:46
  144.7 9.3 %fusion.8 = f32[96,256,128]{2,1,0:T(8,128)} fusion(bf16[96,128,128]{2,1,0:T(8,128)(2,1)S(1)} %copy-done, bf16[96,128,256]{2,1,0:T(8,128)(2,1)} %gather_fusion.3, pred[96]{0:T(512)(128)(4,1)S(1)} %get-tuple-element.11), kind=kOutput, calls=%fused_computation.12 | convolution fusion | flops 808452096 | bytes 22020192 | tf_op jit(solution)/shard_map/sji,sjw->siw/dot_general | solution.py:47
  154.0 12.7 %copy.13 = f32[96,256,128]{1,0,2:T(8,128)} copy(f32[96,256,128]{2,1,0:T(8,128)} %fusion.8) | data formatting | bytes 25165824 | tf_op jit(solution)/shard_map/sji,sjw->siw/dot_general | solution.py:47
  166.7 7.1 %fusion.27 = bf16[16,128,256]{2,0,1:T(8,128)(2,1)S(1)} fusion(f32[96,256,128]{1,0,2:T(8,128)} %copy.13, s32[96]{0:T(128)S(1)} %copy-done.9, pred[96]{0:T(512)(128)(4,1)S(1)} %iota_compare_fusion.2), kind=kOutput, calls=%fused_computation.29 | convolution fusion | flops 604507136 | bytes 13631968 | tf_op jit(solution)/shard_map/bs,siw->biw/dot_general | solution.py:50
  173.8 1.4 copy.9
  175.6 7.3 %gather_fusion.2 = bf16[96,128,256]{2,1,0:T(8,128)(2,1)} fusion(bf16[16,128,256]{2,1,0:T(8,128)(2,1)} %bitcast.43, s32[1024]{0:T(1024)S(1)} %pad_clamp_fusion.1), kind=kCustom, calls=%fused_computation.2.clone | custom fusion | bytes 12583296 | tf_op jit(solution)/shard_map/jit(_take)/gather | solution.py:37
  182.8 9.4 %fusion.10 = f32[96,256,128]{2,1,0:T(8,128)} fusion(bf16[96,128,128]{2,1,0:T(8,128)(2,1)S(1)} %copy-done, bf16[96,128,256]{2,1,0:T(8,128)(2,1)} %gather_fusion.2, pred[96]{0:T(512)(128)(4,1)S(1)} %copy-done.7), kind=kOutput, calls=%fused_computation.14 | convolution fusion | flops 808452096 | bytes 22020192 | tf_op jit(solution)/shard_map/sij,sjw->siw/dot_general | solution.py:38
  192.2 12.8 %copy.12 = f32[96,256,128]{1,0,2:T(8,128)} copy(f32[96,256,128]{2,1,0:T(8,128)} %fusion.10) | data formatting | bytes 25165824 | tf_op jit(solution)/shard_map/sij,sjw->siw/dot_general | solution.py:38
  205.1 7.0 %fusion.33 = bf16[8,128,256]{2,0,1:T(8,128)(2,1)S(1)} fusion(f32[96,256,128]{1,0,2:T(8,128)} %copy.12, s32[96]{0:T(128)S(1)} %copy-done.5, pred[96]{0:T(512)(128)(4,1)S(1)} %iota_compare_fusion.2), kind=kOutput, calls=%fused_computation.31 | convolution fusion | flops 302253568 | bytes 13107680 | tf_op jit(solution)/shard_map/as,siw->aiw/dot_general | solution.py:39
  212.1 0.9 copy.8
  213.1 20.3 %reduce-scatter.9.cloned.1.call-done = bf16[256,256]{1,0:T(8,128)(2,1)} async-done(((bf16[1024,256]{1,0:T(8,128)(2,1)}), bf16[256,256]{1,0:T(8,128)(2,1)}) %reduce-scatter.9.cloned.1.call-update) | async-done | bytes 131088 | tf_op jit(solution)/shard_map/reduce_scatter | solution.py:42
  233.4 1.7 fusion.39
  (56 shorter events, 8.4 us)
Async XLA Ops:
  6.5 24.1 %copy-start = (bf16[96,128,128]{2,1,0:T(8,128)(2,1)S(1)}, bf16[96,128,128]{2,1,0:T(8,128)(2,1)}, u32[]{:S(2)}) copy-start(bf16[96,128,128]{2,1,0:T(8,128)(2,1)} %param.10) | copy-start | bytes 9437188
  6.5 54.9 %all-gather.3.cloned.1.call-start = ((), (), s32[]{:S(2)}) async-start(), calls=%async_computation.4 | async-start | bytes 1179648 | tf_op jit(solution)/shard_map/all_gather | solution.py:36
  6.5 9.7 %collective-permute-start = (bf16[256,256]{1,0:T(8,128)(2,1)}, bf16[256,256]{1,0:T(8,128)(2,1)S(1)}, u32[]{:S(2)}, u32[]{:S(2)}) collective-permute-start(bf16[256,256]{1,0:T(8,128)(2,1)} %param.9), channel_id=1, source_target_pairs={{0,1},{1,2},{2,3},{3,0},{4,5},{5,6},{6,7},{7,4},{8,9},{9,10},{10,1... | collective-permute-start | bytes 393224 | tf_op jit(solution)/shard_map/ppermute | solution.py:20
  9.6 8.0 %collective-permute-start.1 = (bf16[256,256]{1,0:T(8,128)(2,1)}, bf16[256,256]{1,0:T(8,128)(2,1)S(1)}, u32[]{:S(2)}, u32[]{:S(2)}) collective-permute-start(bf16[256,256]{1,0:T(8,128)(2,1)} %param.9), channel_id=1, source_target_pairs={{0,3},{1,0},{2,1},{3,2},{4,7},{5,4},{6,5},{7,6},{8,11},{9,8},{10,9... | collective-permute-start | bytes 393224 | tf_op jit(solution)/shard_map/ppermute | solution.py:25
  11.6 87.4 %reduce-scatter.7.cloned.1.call-start = ((), (), s32[]{:S(2)}) async-start(), calls=%async_computation.6 | async-start | bytes 1179648 | tf_op jit(solution)/shard_map/reduce_scatter | solution.py:53
  12.4 78.6 %copy-start.4 = (s32[96]{0:T(128)}, s32[96]{0:T(128)S(1)}, u32[]{:S(2)}) copy-start(s32[96]{0:T(128)S(1)} %get-tuple-element.12) | copy-start | bytes 1156
  13.1 48.3 %copy-start.8 = (s32[96]{0:T(128)}, s32[96]{0:T(128)S(1)}, u32[]{:S(2)}) copy-start(s32[96]{0:T(128)S(1)} %get-tuple-element.10) | copy-start | bytes 1156
  13.1 55.7 %copy-start.6 = (pred[96]{0:T(512)(128)(4,1)}, pred[96]{0:T(512)(128)(4,1)S(1)}, u32[]{:S(2)}) copy-start(pred[96]{0:T(512)(128)(4,1)S(1)} %get-tuple-element.9) | copy-start | bytes 292
  16.2 6.8 %collective-permute-start.2 = (bf16[256,256]{1,0:T(8,128)(2,1)S(1)}, bf16[256,256]{1,0:T(8,128)(2,1)S(1)}, u32[]{:S(2)}, u32[]{:S(2)}) collective-permute-start(bf16[256,256]{1,0:T(8,128)(2,1)S(1)} %collective-permute-done), channel_id=1, source_target_pairs={{0,1},{1,2},{2,3},{3,0},{4,5},{5,6},{6,7},{7,4},{8,9},{9,10},{10,1... | collective-permute-start | bytes 393224 | tf_op jit(solution)/shard_map/ppermute | solution.py:20
  61.1 59.7 %reduce-scatter.5.cloned.1.call-start = ((), (), s32[]{:S(2)}) async-start(), calls=%async_computation.5 | async-start | bytes 655360 | tf_op jit(solution)/shard_map/reduce_scatter | solution.py:42
  90.9 30.7 %copy-start.1 = (bf16[256,256]{1,0:T(8,128)(2,1)S(1)}, bf16[256,256]{1,0:T(8,128)(2,1)}, u32[]{:S(2)}) copy-start(bf16[256,256]{1,0:T(8,128)(2,1)} %param.9) | copy-start | bytes 393220
  99.0 76.5 %all-gather.5.cloned.1.call-start = ((), (), s32[]{:S(2)}) async-start(), calls=%async_computation.7 | async-start | bytes 1179648 | tf_op jit(solution)/shard_map/all_gather | solution.py:36
  123.3 0.7 copy-start.2
  123.3 7.0 %collective-permute-start.3 = (bf16[256,256]{1,0:T(8,128)(2,1)S(1)}, bf16[256,256]{1,0:T(8,128)(2,1)S(1)}, u32[]{:S(2)}, u32[]{:S(2)}) collective-permute-start(bf16[256,256]{1,0:T(8,128)(2,1)S(1)} %get-tuple-element.8), channel_id=1, source_target_pairs={{0,1},{1,2},{2,3},{3,0},{4,5},{5,6},{6,7},{7,4},{8,9},{9,10},{10,1... | collective-permute-start | bytes 393224 | tf_op jit(solution)/shard_map/ppermute | solution.py:20
  124.0 89.0 %reduce-scatter.11.cloned.1.call-start = ((), (), s32[]{:S(2)}) async-start(), calls=%async_computation.9 | async-start | bytes 1179648 | tf_op jit(solution)/shard_map/reduce_scatter | solution.py:53
  124.1 6.9 %collective-permute-start.4 = (bf16[256,256]{1,0:T(8,128)(2,1)}, bf16[256,256]{1,0:T(8,128)(2,1)S(1)}, u32[]{:S(2)}, u32[]{:S(2)}) collective-permute-start(bf16[256,256]{1,0:T(8,128)(2,1)} %copy-done.2), channel_id=1, source_target_pairs={{0,3},{1,0},{2,1},{3,2},{4,7},{5,4},{6,5},{7,6},{8,11},{9,8},{10,9... | collective-permute-start | bytes 393224 | tf_op jit(solution)/shard_map/ppermute | solution.py:25
  130.3 6.8 %collective-permute-start.5 = (bf16[256,256]{1,0:T(8,128)(2,1)S(1)}, bf16[256,256]{1,0:T(8,128)(2,1)S(1)}, u32[]{:S(2)}, u32[]{:S(2)}) collective-permute-start(bf16[256,256]{1,0:T(8,128)(2,1)S(1)} %collective-permute-done.3), channel_id=1, source_target_pairs={{0,1},{1,2},{2,3},{3,0},{4,5},{5,6},{6,7},{7,4},{8,9},{9,10},{10,1... | collective-permute-start | bytes 393224 | tf_op jit(solution)/shard_map/ppermute | solution.py:20
  154.0 12.7 %copy-start.9 = (s32[96]{0:T(128)S(1)}, s32[96]{0:T(128)}, u32[]{:S(2)}) copy-start(s32[96]{0:T(128)} %copy-done.8) | copy-start | bytes 1156
  175.2 58.2 %reduce-scatter.9.cloned.1.call-start = ((), (), s32[]{:S(2)}) async-start(), calls=%async_computation.8 | async-start | bytes 655360 | tf_op jit(solution)/shard_map/reduce_scatter | solution.py:42
  175.5 7.3 %copy-start.7 = (pred[96]{0:T(512)(128)(4,1)S(1)}, pred[96]{0:T(512)(128)(4,1)}, u32[]{:S(2)}) copy-start(pred[96]{0:T(512)(128)(4,1)} %copy-done.6) | copy-start | bytes 292
  192.2 12.8 %copy-start.5 = (s32[96]{0:T(128)S(1)}, s32[96]{0:T(128)}, u32[]{:S(2)}) copy-start(s32[96]{0:T(128)} %copy-done.4) | copy-start | bytes 1156
  205.1 28.3 %copy-start.3 = (bf16[256,256]{1,0:T(8,128)(2,1)S(1)}, bf16[256,256]{1,0:T(8,128)(2,1)}, u32[]{:S(2)}) copy-start(bf16[256,256]{1,0:T(8,128)(2,1)} %copy-done.2) | copy-start | bytes 393220
Sparse Core Ops, SparseCore 0:
  11.8 23.5 all-gather.2
  61.3 35.3 reduce-scatter.6
  99.1 21.6 reduce-scatter.4
  124.1 23.9 all-gather.4
  175.3 34.0 reduce-scatter.10
  213.2 20.1 reduce-scatter.8
